TPU v7x, 128 devices: a whole 4x4x4 slice. The times are simulated.
128 devices in a mesh: lon: 16 (over y_lo, x, core), lat: 8 (over z, y_hi).
Axes of the slice: x: 4, y: 4 (y_hi: 2, y_lo: 2; y = y_hi * 2 + y_lo), z: 4, core: 2. Of those that a mesh axis runs over, the one named last changes fastest.
Arguments:
- courant_east: float32 [72, 512, 2048], P(None, 'lat', 'lon'), may hold values from -0.4 to 0.4
- courant_north: float32 [72, 512, 2048], P(None, 'lat', 'lon'), may hold values from -0.4 to 0.4
- obs_cells: int32 [8, 16, 1024], P('lat', 'lon'), may hold values from 0 to 8191
- misfit: float32 [5, 8, 16, 1024], P(None, 'lat', 'lon'), may hold values from -6 to 6
- kernel: float32 [72], replicated, may hold values from 0.25 to 1.75
- ensemble: bfloat16 [64, 512, 2048], P(None, 'lat', 'lon'), may hold values from -0.75 to 0.75
- pair_src: int32 [131072], P(('lon', 'lat')), may hold values from 0 to 4095
- pair_dst: int32 [131072], P(('lon', 'lat')), may hold values from 0 to 4095, as said below
- taper: float32 [131072], P(('lon', 'lat')), may hold values from 0.1 to 1
- var_scale: float32 [512, 2048], P('lat', 'lon'), may hold values from 0.3 to 3
Outputs:
- adjoint_field: float32 [72, 512, 2048], P(None, 'lat', 'lon')
- prior_grad: float32 [512, 2048], P('lat', 'lon')
Inputs may be any that keep to these rules, and one draw needn't show every extreme that they name: `obs_cells`: each index names a cell of its own tile. `pair_dst`: block numbers; among the 1024 pairs of one device at most 64 name blocks of one tile, and some tile gets exactly 64 of them.
All inputs are finite; a program needn't handle non-finite values.
Results may differ from a plain program's by a relative error of at most 0.004.
Values sent between devices are 32-bit elements; how exact they have to be, the bound alone decides.
A program may use at most 128 MiB of HBM per device.

v0:
```python
import jax
import jax.numpy as jnp
from jax import lax
from jax.sharding import PartitionSpec as P

BLK = 16


def passed_along(block, axis, distance):
    devices = range(lax.axis_size(axis))
    route = [((i - distance) % len(devices), i) for i in devices]
    return lax.ppermute(block, axis, route)


def from_behind(value, axis, steps):
    count = lax.axis_size(axis)
    initial, last = (max(0, -steps), min(count, count - steps))
    return lax.ppermute(value, axis, [(source, source + steps) for source in range(initial, last)])


def with_halo(block, sides, width):
    for axis, dim in sides:
        count = lax.axis_size(axis)
        forward = [(i, i + 1) for i in range(count - 1)]
        forward.append((count - 1, 0))
        backward = [(target, source) for source, target in forward]
        low = lax.ppermute(
            lax.slice_in_dim(block, block.shape[dim] - width, None, axis=dim), axis, forward
        )
        high = lax.ppermute(lax.slice_in_dim(block, 0, width, axis=dim), axis, backward)
        block = jnp.concatenate([low, block, high], axis=dim)
    return block


def per_device(
    courant_east,
    courant_north,
    obs_cells,
    misfit,
    kernel,
    ensemble,
    pair_src,
    pair_dst,
    taper,
    var_scale,
):
    levels, tile_lat, tile_lon = courant_east.shape
    lat_count = lax.axis_size("lat")
    lon_count = lax.axis_size("lon")
    rows_global = lax.axis_index("lat") * tile_lat + jnp.arange(tile_lat, dtype=jnp.int32)
    keep_rows = (rows_global < tile_lat * lat_count - 1)[None, :, None]
    north_face = jnp.where(keep_rows, courant_north, 0.0)
    pos_east = jnp.maximum(courant_east, 0.0)
    pos_north = jnp.maximum(north_face, 0.0)
    neg_east = jnp.minimum(courant_east, 0.0)
    neg_north = jnp.minimum(north_face, 0.0)
    west_column = passed_along(neg_east[:, :, -1:], "lon", 1)
    neg_west = jnp.concatenate([west_column, neg_east[:, :, :-1]], axis=2)
    south_row = from_behind(neg_north[:, -1:, :], "lat", 1)
    neg_south = jnp.concatenate([south_row, neg_north[:, :-1, :]], axis=1)
    flat_cells = obs_cells.reshape(-1)

    def forcing(step_index):
        column = (
            jnp.zeros((tile_lat * tile_lon,), jnp.float32)
            .at[flat_cells]
            .add(misfit[step_index].reshape(-1))
        )
        return kernel[:, None, None] * column.reshape(tile_lat, tile_lon)[None]

    adj_field = forcing(0)
    surface = adj_field[0]
    for step_index in range(1, misfit.shape[0]):
        padded = with_halo(adj_field, (("lat", 1), ("lon", 2)), 1)
        east_vals = padded[:, 1:-1, 2:]
        west_vals = padded[:, 1:-1, :-2]
        north_vals = padded[:, 2:, 1:-1]
        south_vals = padded[:, :-2, 1:-1]
        adj_field = (
            adj_field
            + pos_east * (east_vals - adj_field)
            + neg_west * (adj_field - west_vals)
            + pos_north * (north_vals - adj_field)
            + neg_south * (adj_field - south_vals)
            + forcing(step_index)
        )
        surface = surface + adj_field[0]
    members = ensemble.shape[0]
    block_rows = tile_lat // BLK
    block_cols = tile_lon // BLK
    own_blocks = block_rows * block_cols
    ens_blocks = ensemble.reshape(members, block_rows, BLK, block_cols, BLK)
    grad_blocks = surface.astype(jnp.bfloat16).reshape(block_rows, BLK, block_cols, BLK)
    local_coeffs = jnp.einsum(
        "mrpcq,rpcq->rcm", ens_blocks, grad_blocks, preferred_element_type=jnp.float32
    ).reshape(own_blocks, members)
    device_count = lon_count * lat_count
    total_blocks = own_blocks * device_count
    all_coeffs = lax.all_gather(local_coeffs, ("lon", "lat"), axis=0, tiled=True)
    partial_sums = jax.ops.segment_sum(
        taper[:, None] * all_coeffs[pair_src], pair_dst, num_segments=total_blocks
    )
    combined = lax.psum_scatter(partial_sums, ("lon", "lat"), scatter_dimension=0, tiled=True)
    combined16 = combined.astype(jnp.bfloat16).reshape(block_rows, block_cols, members)
    field_part = jnp.einsum(
        "mrpcq,rcm->rpcq", ens_blocks, combined16, preferred_element_type=jnp.float32
    ).reshape(tile_lat, tile_lon)
    prior_grad = var_scale * surface + field_part
    return (adj_field, prior_grad)


def solution(mesh):
    in_specs = (
        P(None, "lat", "lon"),
        P(None, "lat", "lon"),
        P("lat", "lon", None),
        P(None, "lat", "lon", None),
        P(),
        P(None, "lat", "lon"),
        P(("lon", "lat")),
        P(("lon", "lat")),
        P(("lon", "lat")),
        P("lat", "lon"),
    )
    out_specs = (P(None, "lat", "lon"), P("lat", "lon"))
    return jax.shard_map(
        per_device, mesh=mesh, in_specs=in_specs, out_specs=out_specs, check_vma=False
    )
```

profile of v0, /device:TPU:0, one launch (start us, length us, event | category | flops | bytes accessed | tf_op | source)
XLA Modules:
  0.0 1187.5 jit_solution(14152861951485718959)
XLA Ops:
  7.2 1.3 fusion.79
  9.3 5.9 scatter_custom_fusion
  15.2 0.9 broadcast_multiply_fusion
  16.1 1.4 copy-done.3
  17.5 3.4 collective-permute-start
  20.9 3.6 collective-permute-start.1
  24.5 2.2 select_minimum_fusion
  26.7 1.9 collective-permute-start.5
  29.0 3.1 fusion.74
  32.2 2.5 copy.20
  34.7 1.5 collective-permute-start.2
  36.2 2.5 copy.24
  38.8 1.9 broadcast_minimum_fusion
  40.7 1.4 copy-done.5
  42.1 2.1 slice.205
  44.2 2.8 copy.22
  47.2 6.5 scatter_custom_fusion.1
  53.7 3.2 copy.23
  56.8 2.4 copy.21
  59.3 2.4 copy.25
  61.6 12.2 %fusion.4 = (f32[72,64,128]{2,1,0:T(8,128)S(1)}, f32[72,64,128]{2,1,0:T(8,128)}) fusion(f32[72,64,128]{2,1,0:T(8,128)} %copy-done.3, f32[72,1,128]{2,1,0:T(1,128)S(1)} %collective-permute-done, f32[72,1,128]{2,1,0:T(1,128)S(1)} %collective-permute-done.1, f32[72,66,1]{2,1,0:T(8,128)} %copy.25, f32[72,66,1]{2,1,0:T(8,128)} %copy.21, ...), kind=kLoop, calls=%fused_computation.20 | loop fusion | flops 16515072 | bytes 16692704 | tf_op jit(solution)/shard_map/add | solution.py:80
  73.9 4.0 collective-permute-start.6
  77.9 1.7 collective-permute-start.7
  79.6 1.9 collective-permute-done.6
  81.5 1.9 collective-permute-done.7
  83.8 3.1 fusion.73
  87.0 2.5 copy.26
  89.5 2.0 collective-permute-start.8
  91.5 2.5 copy.28
  94.1 6.1 scatter_custom_fusion.2
  100.2 2.4 copy.27
  102.6 2.4 copy.29
  105.0 10.6 fusion.37
  115.6 2.9 collective-permute-start.10
  118.6 2.8 collective-permute-start.11
  121.4 2.3 collective-permute-done.10
  124.5 3.1 fusion.72
  127.6 2.5 copy.30
  130.1 2.0 collective-permute-start.12
  132.1 2.5 copy.32
  134.7 5.9 scatter_custom_fusion.3
  140.7 2.4 copy.31
  143.1 2.4 copy.33
  145.5 11.0 fusion.24
  156.5 4.1 collective-permute-start.14
  160.7 2.2 collective-permute-start.15
  162.9 2.0 collective-permute-done.14
  164.9 1.2 collective-permute-done.15
  166.6 3.2 fusion.71
  169.7 3.2 copy.34
  173.0 1.8 collective-permute-start.16
  174.8 3.1 copy.36
  177.9 6.1 scatter_custom_fusion.4
  184.0 2.3 copy.38
  186.3 3.1 copy.35
  189.4 3.2 copy.37
  192.6 10.8 fusion.11
  203.4 1.4 copy-done.7
  204.8 0.8 fusion.70
  205.8 2.8 fusion.49
  208.9 302.3 %all-gather.2.cloned.1.call-done = f32[4096,64]{1,0:T(8,128)} async-done(((f32[32,64]{1,0:T(8,128)}), f32[4096,64]{1,0:T(8,128)}) %all-gather.2.cloned.1.call-update) | async-done | bytes 1048592 | tf_op jit(solution)/shard_map/all_gather | solution.py:99
  511.2 13.8 %scatter_custom_fusion.5 = f32[4096,64]{1,0:T(8,128)} fusion(s32[1024]{0:T(1024)} %param.17, f32[]{:T(128)} %constant.7.clone.1, f32[1024]{0:T(1024)S(1)} %copy-done.14, f32[4096,64]{1,0:T(8,128)} %all-gather.2.cloned.1.call-done, s32[1024]{0:T(1024)S(1)} %fusion.68), kind=kCustom, calls=%fused_computation.105 | custom fusion | flops 131072 | bytes 3154432 | tf_op jit(solution)/shard_map/scatter-add | solution.py:100
  525.0 648.7 %reduce-scatter.2.cloned.1.call-done = f32[32,64]{1,0:T(8,128)} async-done(((f32[4096,64]{1,0:T(8,128)}), f32[32,64]{1,0:T(8,128)}) %reduce-scatter.2.cloned.1.call-update) | async-done | bytes 8208 | tf_op jit(solution)/shard_map/reduce_scatter | solution.py:103
  1174.4 4.9 fusion.47
  (66 shorter events, 5.6 us)
Async XLA Ops:
  7.2 504.0 %all-gather.2.cloned.1.call-start = ((), (), s32[]{:S(2)}) async-start(), calls=%async_computation.1 | async-start | bytes 2113536 | tf_op jit(solution)/shard_map/all_gather | solution.py:99
  9.2 125.5 %copy-start.13 = (s32[1024,1]{0,1:T(1,128)}, s32[1024,1]{0,1:T(1,128)S(1)}, u32[]{:S(2)}) copy-start(s32[1024,1]{0,1:T(1,128)S(1)} %compare_select_fusion) | copy-start | bytes 12292
  16.1 1.4 copy-start.3
  17.5 11.0 collective-permute-start
  20.9 7.7 collective-permute-start.1
  24.5 4.1 copy-start.4
  26.7 35.0 %collective-permute-start.5 = (f32[72,1,128]{2,1,0:T(1,128)S(1)}, f32[72,1,128]{2,1,0:T(1,128)S(1)}, u32[]{:S(2)}, u32[]{:S(2)}) collective-permute-start(f32[72,1,128]{2,1,0:T(1,128)S(1)} %slice.208), channel_id=1, source_target_pairs={{0,1},{1,2},{2,3},{3,4},{4,5},{5,6},{6,7},{8,9},{9,10},{10,11},{11... | collective-permute-start | bytes 110600 | tf_op jit(solution)/shard_map/ppermute | solution.py:18
  34.7 22.1 %collective-permute-start.2 = (f32[72,66,1]{0,2,1:T(1,128)S(1)}, f32[72,66,1]{0,2,1:T(1,128)S(1)}, u32[]{:S(2)}, u32[]{:S(2)}) collective-permute-start(f32[72,66,1]{0,2,1:T(1,128)S(1)} %copy.20), channel_id=1, source_target_pairs={{8,0},{16,8},{24,16},{32,24},{40,32},{48,40},{56,48},{64,56},{72,6... | collective-permute-start | bytes 57032 | tf_op jit(solution)/shard_map/ppermute | solution.py:30
  38.7 20.5 %collective-permute-start.4 = (f32[72,66,1]{0,2,1:T(1,128)S(1)}, f32[72,66,1]{0,2,1:T(1,128)S(1)}, u32[]{:S(2)}, u32[]{:S(2)}) collective-permute-start(f32[72,66,1]{0,2,1:T(1,128)S(1)} %copy.24), channel_id=1, source_target_pairs={{0,8},{8,16},{16,24},{24,32},{32,40},{40,48},{48,56},{56,64},{64,7... | collective-permute-start | bytes 57032 | tf_op jit(solution)/shard_map/ppermute | solution.py:27
  40.7 1.4 copy-start.5
  47.0 6.6 collective-permute-start.3
  56.8 4.8 copy-start.10
  73.8 10.0 copy-start
  73.9 7.6 collective-permute-start.6
  77.9 5.5 collective-permute-start.7
  89.5 10.7 collective-permute-start.8
  94.0 8.6 collective-permute-start.9
  115.6 8.9 copy-start.1
  115.6 8.0 collective-permute-start.10
  118.6 5.5 collective-permute-start.11
  130.1 10.6 collective-permute-start.12
  134.7 8.4 collective-permute-start.13
  156.5 10.1 copy-start.2
  156.5 8.3 collective-permute-start.14
  160.7 5.5 collective-permute-start.15
  169.7 14.3 %copy-start.8 = (bf16[64,64,128]{2,1,0:T(8,128)(2,1)S(1)}, bf16[64,64,128]{2,1,0:T(8,128)(2,1)}, u32[]{:S(2)}) copy-start(bf16[64,64,128]{2,1,0:T(8,128)(2,1)} %param.15) | copy-start | bytes 3145732
  173.0 13.3 %collective-permute-start.16 = (f32[72,66,1]{0,2,1:T(1,128)}, f32[72,66,1]{0,2,1:T(1,128)}, u32[]{:S(2)}, u32[]{:S(2)}) collective-permute-start(f32[72,66,1]{0,2,1:T(1,128)} %copy.34), channel_id=1, source_target_pairs={{8,0},{16,8},{24,16},{32,24},{40,32},{48,40},{56,48},{64,56},{72,6... | collective-permute-start | bytes 57032 | tf_op jit(solution)/shard_map/ppermute | solution.py:30
  177.9 11.5 collective-permute-start.17
  186.3 6.3 copy-start.11
  203.4 1.4 copy-start.7
  204.8 4.1 copy-start.12
  204.8 306.4 %copy-start.14 = (f32[1024]{0:T(1024)S(1)}, f32[1024]{0:T(1024)}, u32[]{:S(2)}) copy-start(f32[1024]{0:T(1024)} %param.18) | copy-start | bytes 12292
  208.6 965.1 %reduce-scatter.2.cloned.1.call-start = ((), (), s32[]{:S(2)}) async-start(), calls=%async_computation.2 | async-start | bytes 2113536 | tf_op jit(solution)/shard_map/reduce_scatter | solution.py:103
  208.9 965.5 %copy-start.6 = (bf16[64,64,128]{0,2,1:T(8,128)(2,1)S(1)}, bf16[64,64,128]{0,2,1:T(8,128)(2,1)}, u32[]{:S(2)}) copy-start(bf16[64,64,128]{0,2,1:T(8,128)(2,1)} %copy.38) | copy-start | bytes 3145732
  525.0 654.6 %copy-start.9 = (f32[64,128]{1,0:T(8,128)S(1)}, f32[64,128]{1,0:T(8,128)}, u32[]{:S(2)}) copy-start(f32[64,128]{1,0:T(8,128)} %param.19) | copy-start | bytes 98308
Sparse Core Ops, SparseCore 0:
  208.7 302.4 all-gather.1
  525.1 648.5 reduce-scatter.1
where the time goes:
time: 1200 us; the launch traced here: 1190 us
  waiting for transfers between devices  961 us (80%)
  other arithmetic  98.3 us (8%)
  local copies, waits for them, and re-layouts  71.3 us (6%)
  starting transfers between devices  34.6 us (3%)
  between operations  14.9 us (1%)
    reduce_scatter x1, waiting for transfers between devices, per_device(): lax.psum_scatter(partial_sums, ('lon', 'lat'), scatter_dimension=0, tiled...  649 us
    all_gather x1, waiting for transfers between devices, per_device(): lax.all_gather(local_coeffs, ('lon', 'lat'), axis=0, tiled=True)  302 us
    add x4, other arithmetic, per_device(): adj_field + pos_east * (east_vals - adj_field)  44.5 us
    scatter-add x5, other arithmetic, forcing(): column = jnp.zeros((tile_lat * tile_lon,), jnp.float32).at[flat_cells].ad...  30.5 us
  transfers between devices with their start and end apart: 20, of which 8 were waited for; matrix products, arithmetic and copies ran while one was open for 6% of the time, Pallas kernels for 0%

commit v1 on v0

--- a/solution.py
+++ b/solution.py
@@ -96,7 +96,12 @@
     ).reshape(own_blocks, members)
     device_count = lon_count * lat_count
     total_blocks = own_blocks * device_count
-    all_coeffs = lax.all_gather(local_coeffs, ("lon", "lat"), axis=0, tiled=True)
+    all_coeffs = jnp.concatenate(
+        lax.all_to_all(
+            jnp.stack([local_coeffs] * lax.axis_size(("lon", "lat"))), ("lon", "lat"), 0, 0
+        ),
+        axis=0,
+    )
     partial_sums = jax.ops.segment_sum(
         taper[:, None] * all_coeffs[pair_src], pair_dst, num_segments=total_blocks
     )

time: 1200 us -> 923 us (0.77)
  waiting for transfers between devices: 961 us -> 671 us
    all_gather x1 -> x0, waiting for transfers between devices: 302 us -> none  [per_device(): lax.all_gather(local_coeffs, ('lon', 'lat'), axis=0, tiled=True)]
    all_to_all x0 -> x1, waiting for transfers between devices: none -> 17.8 us  [per_device(): lax.all_to_all(jnp.stack([local_coeffs] * lax.axis_size(('lon', 'lat'))),...]
  transfers between devices with their start and end apart: 20 -> 20, of which waited for: 8 -> 8; matrix products, arithmetic and copies ran while one was open for 6% -> 7% of each run, Pallas kernels for 0% -> 0%
where the time goes in v1:
time: 923 us; the launch traced here: 915 us
  waiting for transfers between devices  671 us (73%)
  other arithmetic  101 us (11%)
  local copies, waits for them, and re-layouts  76.5 us (8%)
  starting transfers between devices  44.1 us (5%)
  between operations  14.6 us (2%)
    reduce_scatter x1, waiting for transfers between devices, per_device(): lax.psum_scatter(partial_sums, ('lon', 'lat'), scatter_dimension=0, tiled...  644 us
    add x4, other arithmetic, per_device(): adj_field + pos_east * (east_vals - adj_field)  44.4 us
    scatter-add x5, other arithmetic, forcing(): column = jnp.zeros((tile_lat * tile_lon,), jnp.float32).at[flat_cells].ad...  30.2 us
    slice x12, local copies, waits for them, and re-layouts, with_halo(): lax.slice_in_dim(block, 0, width, axis=dim)  23.6 us
  transfers between devices with their start and end apart: 20, of which 8 were waited for; matrix products, arithmetic and copies ran while one was open for 7% of the time, Pallas kernels for 0%

profile of v1, /device:TPU:0, one launch (start us, length us, event | category | flops | bytes accessed | tf_op | source)
XLA Modules:
  0.0 915.0 jit_solution(1015964062549016103)
XLA Ops:
  9.2 5.9 scatter_custom_fusion
  16.0 1.4 copy-done.3
  17.5 3.4 collective-permute-start
  20.9 3.6 collective-permute-start.1
  24.4 2.2 select_minimum_fusion
  26.6 1.9 collective-permute-start.5
  29.0 3.1 fusion.74
  32.1 2.5 copy.20
  34.7 1.5 collective-permute-start.2
  36.2 2.5 copy.24
  38.8 1.9 broadcast_minimum_fusion
  40.7 1.4 copy-done.5
  42.1 2.1 slice.205
  44.2 2.8 copy.22
  47.2 6.1 scatter_custom_fusion.1
  53.3 3.2 copy.23
  56.5 2.4 copy.21
  58.9 2.4 copy.25
  61.3 12.2 %fusion.4 = (f32[72,64,128]{2,1,0:T(8,128)S(1)}, f32[72,64,128]{2,1,0:T(8,128)}) fusion(f32[72,64,128]{2,1,0:T(8,128)} %copy-done.3, f32[72,1,128]{2,1,0:T(1,128)S(1)} %collective-permute-done, f32[72,1,128]{2,1,0:T(1,128)S(1)} %collective-permute-done.1, f32[72,66,1]{2,1,0:T(8,128)} %copy.25, f32[72,66,1]{2,1,0:T(8,128)} %copy.21, ...), kind=kLoop, calls=%fused_computation.20 | loop fusion | flops 16515072 | bytes 16692704 | tf_op jit(solution)/shard_map/add | solution.py:80
  73.5 4.0 collective-permute-start.6
  77.6 1.7 collective-permute-start.7
  79.2 1.9 collective-permute-done.6
  81.2 1.9 collective-permute-done.7
  83.5 3.1 fusion.73
  86.6 2.5 copy.26
  89.1 2.0 collective-permute-start.8
  91.1 2.5 copy.28
  93.7 6.2 scatter_custom_fusion.2
  99.9 2.4 copy.27
  102.3 2.4 copy.29
  104.7 10.7 %fusion.37 = f32[72,64,128]{2,1,0:T(8,128)S(1)} fusion(f32[72,64,128]{2,1,0:T(8,128)} %copy-done, f32[72,1,128]{2,1,0:T(1,128)S(1)} %collective-permute-done.6, f32[72,1,128]{2,1,0:T(1,128)S(1)} %collective-permute-done.7, f32[72,64,128]{2,1,0:T(8,128)} %get-tuple-element.7, f32[72,66,1]{2,1,0:T(8,128)} %copy.29, f32[72,66,1]{2,1,0:T(8,128)} %copy.27, ...), kind=kLoop, calls=%fused_computation.70 | loop fusion | flops 15335424 | bytes 14300640 | tf_op jit(solution)/shard_map/add | solution.py:80
  115.4 2.9 collective-permute-start.10
  118.4 2.8 collective-permute-start.11
  121.2 2.3 collective-permute-done.10
  124.3 3.1 fusion.72
  127.4 2.5 copy.30
  129.9 2.0 collective-permute-start.12
  131.9 2.5 copy.32
  134.5 5.9 scatter_custom_fusion.3
  140.5 2.4 copy.31
  142.9 2.4 copy.33
  145.3 10.9 %fusion.24 = f32[72,64,128]{2,1,0:T(8,128)S(1)} fusion(f32[72,64,128]{2,1,0:T(8,128)} %copy-done.1, f32[72,1,128]{2,1,0:T(1,128)S(1)} %collective-permute-done.10, f32[72,1,128]{2,1,0:T(1,128)S(1)} %collective-permute-done.11, f32[72,64,128]{2,1,0:T(8,128)} %get-tuple-element.7, f32[72,66,1]{2,1,0:T(8,128)} %copy.33, f32[72,66,1]{2,1,0:T(8,128)} %copy.31, ...), kind=kLoop, calls=%fused_computation.49 | loop fusion | flops 15335424 | bytes 14300640 | tf_op jit(solution)/shard_map/add | solution.py:80
  156.3 4.3 collective-permute-start.14
  160.6 2.2 collective-permute-start.15
  162.8 2.0 collective-permute-done.14
  166.5 3.2 fusion.71
  169.7 3.2 copy.34
  172.9 1.8 collective-permute-start.16
  174.7 3.1 copy.36
  177.8 6.1 scatter_custom_fusion.4
  183.9 2.3 copy.38
  186.2 3.1 copy.35
  189.3 3.2 copy.37
  192.5 10.7 %fusion.11 = f32[72,64,128]{2,1,0:T(8,128)S(1)} fusion(f32[72,64,128]{2,1,0:T(8,128)} %copy-done.2, f32[72,1,128]{2,1,0:T(1,128)S(1)} %collective-permute-done.14, f32[72,1,128]{2,1,0:T(1,128)S(1)} %collective-permute-done.15, f32[72,64,128]{2,1,0:T(8,128)} %get-tuple-element.7, f32[72,66,1]{2,1,0:T(8,128)} %copy.37, f32[72,66,1]{2,1,0:T(8,128)} %copy.35, ...), kind=kLoop, calls=%fused_computation.28 | loop fusion | flops 15335424 | bytes 14300640 | tf_op jit(solution)/shard_map/add | solution.py:80
  203.2 1.4 copy-done.7
  205.5 2.2 fusion.49
  208.0 2.3 reshape.164
  210.3 9.5 %all-to-all-start = ((f32[128,1,2048]{2,1,0:T(1,128)}), f32[128,1,2048]{2,1,0:T(1,128)S(1)}, u32[]{:S(2)}, u32[]{:S(2)}) async-start(f32[128,1,2048]{2,1,0:T(1,128)} %reshape.164), calls=%async_computation | async-start | bytes 2097152 | tf_op jit(solution)/shard_map/all_to_all | solution.py:100
  220.1 17.8 %all-to-all-done = f32[128,1,2048]{2,1,0:T(1,128)S(1)} async-done(((f32[128,1,2048]{2,1,0:T(1,128)}), f32[128,1,2048]{2,1,0:T(1,128)S(1)}, u32[]{:S(2)}, u32[]{:S(2)}) %all-to-all-start) | async-done | bytes 1048608 | tf_op jit(solution)/shard_map/all_to_all | solution.py:100
  238.3 3.1 reduce
  241.5 2.1 reshape.165
  243.6 13.9 %scatter_custom_fusion.5 = f32[4096,64]{1,0:T(8,128)} fusion(s32[1024]{0:T(1024)} %param.17, f32[]{:T(128)} %constant.7.clone.1, f32[1024]{0:T(1024)S(1)} %copy-done.14, f32[4096,64]{1,0:T(8,128)} %bitcast.44, s32[1024]{0:T(1024)S(1)} %fusion.68), kind=kCustom, calls=%fused_computation.105 | custom fusion | flops 131072 | bytes 3154432 | tf_op jit(solution)/shard_map/scatter-add | solution.py:105
  257.6 643.8 %reduce-scatter.2.cloned.1.call-done = f32[32,64]{1,0:T(8,128)} async-done(((f32[4096,64]{1,0:T(8,128)}), f32[32,64]{1,0:T(8,128)}) %reduce-scatter.2.cloned.1.call-update) | async-done | bytes 8208 | tf_op jit(solution)/shard_map/reduce_scatter | solution.py:108
  902.1 4.9 fusion.47
  (70 shorter events, 10.5 us)
Async XLA Ops:
  9.2 125.3 %copy-start.13 = (s32[1024,1]{0,1:T(1,128)}, s32[1024,1]{0,1:T(1,128)S(1)}, u32[]{:S(2)}) copy-start(s32[1024,1]{0,1:T(1,128)S(1)} %compare_select_fusion) | copy-start | bytes 12292
  16.0 1.4 copy-start.3
  17.5 11.0 %collective-permute-start = (f32[72,1,128]{2,1,0:T(1,128)S(1)}, f32[72,1,128]{2,1,0:T(1,128)S(1)}, u32[]{:S(2)}, u32[]{:S(2)}) collective-permute-start(f32[72,1,128]{2,1,0:T(1,128)S(1)} %get-tuple-element.23), channel_id=1, source_target_pairs={{0,1},{1,2},{2,3},{3,4},{4,5},{5,6},{6,7},{7,0},{8,9},{9,10},{10,1... | collective-permute-start | bytes 110600 | tf_op jit(solution)/shard_map/ppermute | solution.py:27
  20.9 7.7 collective-permute-start.1
  24.4 4.1 copy-start.4
  26.6 34.6 %collective-permute-start.5 = (f32[72,1,128]{2,1,0:T(1,128)S(1)}, f32[72,1,128]{2,1,0:T(1,128)S(1)}, u32[]{:S(2)}, u32[]{:S(2)}) collective-permute-start(f32[72,1,128]{2,1,0:T(1,128)S(1)} %slice.208), channel_id=1, source_target_pairs={{0,1},{1,2},{2,3},{3,4},{4,5},{5,6},{6,7},{8,9},{9,10},{10,11},{11... | collective-permute-start | bytes 110600 | tf_op jit(solution)/shard_map/ppermute | solution.py:18
  34.7 21.8 %collective-permute-start.2 = (f32[72,66,1]{0,2,1:T(1,128)S(1)}, f32[72,66,1]{0,2,1:T(1,128)S(1)}, u32[]{:S(2)}, u32[]{:S(2)}) collective-permute-start(f32[72,66,1]{0,2,1:T(1,128)S(1)} %copy.20), channel_id=1, source_target_pairs={{8,0},{16,8},{24,16},{32,24},{40,32},{48,40},{56,48},{64,56},{72,6... | collective-permute-start | bytes 57032 | tf_op jit(solution)/shard_map/ppermute | solution.py:30
  38.7 20.2 %collective-permute-start.4 = (f32[72,66,1]{0,2,1:T(1,128)S(1)}, f32[72,66,1]{0,2,1:T(1,128)S(1)}, u32[]{:S(2)}, u32[]{:S(2)}) collective-permute-start(f32[72,66,1]{0,2,1:T(1,128)S(1)} %copy.24), channel_id=1, source_target_pairs={{0,8},{8,16},{16,24},{24,32},{32,40},{40,48},{48,56},{56,64},{64,7... | collective-permute-start | bytes 57032 | tf_op jit(solution)/shard_map/ppermute | solution.py:27
  40.7 1.4 copy-start.5
  47.0 6.3 collective-permute-start.3
  56.5 4.8 copy-start.10
  73.5 10.0 %copy-start = (f32[72,64,128]{2,1,0:T(8,128)}, f32[72,64,128]{2,1,0:T(8,128)S(1)}, u32[]{:S(2)}) copy-start(f32[72,64,128]{2,1,0:T(8,128)S(1)} %get-tuple-element.6) | copy-start | bytes 7077892
  73.5 7.6 collective-permute-start.6
  77.6 5.5 collective-permute-start.7
  89.1 10.8 %collective-permute-start.8 = (f32[72,66,1]{0,2,1:T(1,128)S(1)}, f32[72,66,1]{0,2,1:T(1,128)S(1)}, u32[]{:S(2)}, u32[]{:S(2)}) collective-permute-start(f32[72,66,1]{0,2,1:T(1,128)S(1)} %copy.26), channel_id=1, source_target_pairs={{8,0},{16,8},{24,16},{32,24},{40,32},{48,40},{56,48},{64,56},{72,6... | collective-permute-start | bytes 57032 | tf_op jit(solution)/shard_map/ppermute | solution.py:30
  93.7 8.7 collective-permute-start.9
  115.4 8.9 copy-start.1
  115.4 8.0 collective-permute-start.10
  118.4 5.5 collective-permute-start.11
  129.9 10.6 %collective-permute-start.12 = (f32[72,66,1]{0,2,1:T(1,128)S(1)}, f32[72,66,1]{0,2,1:T(1,128)S(1)}, u32[]{:S(2)}, u32[]{:S(2)}) collective-permute-start(f32[72,66,1]{0,2,1:T(1,128)S(1)} %copy.30), channel_id=1, source_target_pairs={{8,0},{16,8},{24,16},{32,24},{40,32},{48,40},{56,48},{64,56},{72,6... | collective-permute-start | bytes 57032 | tf_op jit(solution)/shard_map/ppermute | solution.py:30
  134.5 8.4 collective-permute-start.13
  156.2 10.3 %copy-start.2 = (f32[72,64,128]{2,1,0:T(8,128)}, f32[72,64,128]{2,1,0:T(8,128)S(1)}, u32[]{:S(2)}) copy-start(f32[72,64,128]{2,1,0:T(8,128)S(1)} %fusion.24) | copy-start | bytes 7077892
  156.3 8.5 collective-permute-start.14
  160.6 5.5 collective-permute-start.15
  169.7 14.3 %copy-start.8 = (bf16[64,64,128]{2,1,0:T(8,128)(2,1)S(1)}, bf16[64,64,128]{2,1,0:T(8,128)(2,1)}, u32[]{:S(2)}) copy-start(bf16[64,64,128]{2,1,0:T(8,128)(2,1)} %param.15) | copy-start | bytes 3145732
  172.9 13.3 %collective-permute-start.16 = (f32[72,66,1]{0,2,1:T(1,128)}, f32[72,66,1]{0,2,1:T(1,128)}, u32[]{:S(2)}, u32[]{:S(2)}) collective-permute-start(f32[72,66,1]{0,2,1:T(1,128)} %copy.34), channel_id=1, source_target_pairs={{8,0},{16,8},{24,16},{32,24},{40,32},{48,40},{56,48},{64,56},{72,6... | collective-permute-start | bytes 57032 | tf_op jit(solution)/shard_map/ppermute | solution.py:30
  177.8 11.5 %collective-permute-start.17 = (f32[72,66,1]{0,2,1:T(1,128)}, f32[72,66,1]{0,2,1:T(1,128)}, u32[]{:S(2)}, u32[]{:S(2)}) collective-permute-start(f32[72,66,1]{0,2,1:T(1,128)} %copy.36), channel_id=1, source_target_pairs={{0,8},{8,16},{16,24},{24,32},{32,40},{40,48},{48,56},{56,64},{64,7... | collective-permute-start | bytes 57032 | tf_op jit(solution)/shard_map/ppermute | solution.py:27
  186.2 6.3 copy-start.11
  203.2 1.4 copy-start.7
  208.0 12.1 %copy-start.12 = (s32[1024]{0:T(1024)S(1)}, s32[1024]{0:T(1024)}, u32[]{:S(2)}) copy-start(s32[1024]{0:T(1024)} %param.16) | copy-start | bytes 12292
  210.3 27.5 %all-to-all-start = ((f32[128,1,2048]{2,1,0:T(1,128)}), f32[128,1,2048]{2,1,0:T(1,128)S(1)}, u32[]{:S(2)}, u32[]{:S(2)}) async-start(f32[128,1,2048]{2,1,0:T(1,128)} %reshape.164), calls=%async_computation | async-start | bytes 2097152 | tf_op jit(solution)/shard_map/all_to_all | solution.py:100
  219.8 681.6 %reduce-scatter.2.cloned.1.call-start = ((), (), s32[]{:S(2)}) async-start(), calls=%async_computation.2 | async-start | bytes 2113536 | tf_op jit(solution)/shard_map/reduce_scatter | solution.py:108
  238.3 5.3 copy-start.14
  243.6 658.5 %copy-start.6 = (bf16[64,64,128]{0,2,1:T(8,128)(2,1)S(1)}, bf16[64,64,128]{0,2,1:T(8,128)(2,1)}, u32[]{:S(2)}) copy-start(bf16[64,64,128]{0,2,1:T(8,128)(2,1)} %copy.38) | copy-start | bytes 3145732
  257.6 649.7 %copy-start.9 = (f32[64,128]{1,0:T(8,128)S(1)}, f32[64,128]{1,0:T(8,128)}, u32[]{:S(2)}) copy-start(f32[64,128]{1,0:T(8,128)} %param.19) | copy-start | bytes 98308
Sparse Core Ops, SparseCore 0:
  257.7 643.6 reduce-scatter.1
